TPU v7x, 512 devices: a whole 4x4x16 slice. The times are simulated.
512 devices in a mesh: row: 16 (over x, y), col: 32 (over z, core).
Axes of the slice: x: 4, y: 4, z: 16, core: 2. Of those that a mesh axis runs over, the one named last changes fastest.
Arguments:
- trail_adjoint: float32 [8, 2048, 4, 4096], P(None, 'row', None, 'col'), may hold values from -6 to 6
- panel: float32 [8, 2048, 128], P(None, 'row'), may hold values from -0.046875 to 0.046875
- panel_adjoint: float32 [8, 2048, 128], P(None, 'row'), may hold values from -6 to 6
- diag_block: float32 [128, 128], replicated, as said below
Outputs:
- input_adjoint: float32 [8, 2048, 128], P(None, 'row')
- block_adjoint: float32 [128, 128], replicated
Inputs may be any that keep to these rules, and one draw needn't show every extreme that they name: diag_block is lower triangular with diagonal entries between 1.5 and 3 and zeros above the diagonal.
All inputs are finite; a program needn't handle non-finite values.
Results may differ from a plain program's by a relative error of at most 0.000082.
Values sent between devices are 32-bit elements; how exact they have to be, the bound alone decides.
A program may use at most 64 MiB of HBM per device.

v0:
```python
import jax
import jax.numpy as jnp
from jax import lax
from jax.sharding import PartitionSpec as P


def spread(value, axis, root):
    mine = lax.axis_index(axis) == root
    return lax.psum(jnp.where(mine, value, jnp.zeros_like(value)), axis)


def solve_rows(total, diag_block):
    return lax.linalg.triangular_solve(diag_block, total, left_side=False, lower=True)


def per_device(trail_adjoint, panel, panel_adjoint, diag_block):
    width = diag_block.shape[0]
    n_row = lax.axis_size("row")
    n_col = lax.axis_size("col")
    ratio = n_col // n_row
    row_blocks = panel.shape[0]
    col_blocks = trail_adjoint.shape[2]
    col_index = lax.axis_index("col")
    row_index = lax.axis_index("row")
    grouped = panel.reshape(col_blocks, ratio, width, width)
    chosen = lax.dynamic_index_in_dim(grouped, col_index // n_row, 1, keepdims=False)
    col_panel = spread(chosen, "row", col_index % n_row)
    flip_part = jnp.einsum(
        "aibj,aik->bjk",
        trail_adjoint,
        panel,
        precision=lax.Precision.HIGHEST,
        preferred_element_type=jnp.float32,
    )
    flip_total = lax.psum(flip_part, "row")
    flat_panel = panel.reshape(row_blocks * width, width)
    flat_given = panel_adjoint.reshape(row_blocks * width, width)
    routed_list = []
    for offset in range(ratio):
        routed_list.append(spread(flip_total, "col", row_index + n_row * offset))
    routed = jnp.stack(routed_list, axis=1).reshape(row_blocks * width, width)
    direct_part = jnp.einsum(
        "aibj,bjk->aik",
        trail_adjoint,
        col_panel,
        precision=lax.Precision.HIGHEST,
        preferred_element_type=jnp.float32,
    )
    direct = lax.psum(direct_part, "col").reshape(row_blocks * width, width)
    total = flat_given - (direct + routed)
    solved = solve_rows(total, diag_block)
    gram_part = -jnp.dot(
        solved.T, flat_panel, precision=lax.Precision.HIGHEST, preferred_element_type=jnp.float32
    )
    gram = lax.psum(gram_part, "row")
    return (solved.reshape(row_blocks, width, width), jnp.tril(gram))


def solution(mesh):
    in_specs = (P(None, "row", None, "col"), P(None, "row", None), P(None, "row", None), P())
    out_specs = (P(None, "row", None), P())
    return jax.shard_map(
        per_device, mesh=mesh, in_specs=in_specs, out_specs=out_specs, check_vma=False
    )
```

profile of v0, /device:TPU:1, one launch (start us, length us, event | category | flops | bytes accessed | tf_op | source)
XLA Modules:
  0.0 477.5 jit_solution(14296262581319625285)
XLA Ops:
  7.2 0.0 copy-start
  7.2 0.0 all-reduce.10.cloned.1.call-start
  7.2 1.0 copy-done
  8.2 0.1 copy.18
  8.4 0.0 copy-start.1
  8.4 5.9 %fusion.7 = f32[4,128,128]{2,1,0:T(8,128)} fusion(f32[8,128,4,128]{3,2,1,0:T(4,128)} %param.4, f32[8,128,128]{2,1,0:T(8,128)S(1)} %copy-done), kind=kOutput, calls=%fused_computation.5 | convolution fusion | flops 805306368 | bytes 2883584 | tf_op jit(solution)/shard_map/aibj,aik->bjk/dot_general | solution.py:28
  14.2 0.7 select_bitcast_fusion.2
  15.0 0.0 all-reduce.10.cloned.1.call-update
  15.0 0.0 all-reduce.8.cloned.1.call-start
  15.0 119.8 %all-reduce.10.cloned.1.call-done = (f32[4,128,128]{1,2,0:T(8,128)}, f32[4,128,128]{2,1,0:T(8,128)}) async-done(((f32[4,128,128]{1,2,0:T(8,128)}, f32[4,128,128]{2,1,0:T(8,128)}), (f32[4,128,128]{1,2,0:T(8,128)}, f32[4,128,128]{2,1,0:T(8,128)})) %all-reduce.10.cloned.1.call-update) | async-done | bytes 524304 | tf_op jit(solution)/shard_map/psum | solution.py:9
  134.9 0.0 copy-start.5
  134.9 0.0 copy-done.1
  134.9 0.0 copy-start.3
  134.9 4.1 fusion.4
  139.0 0.0 copy-start.6
  139.0 0.0 copy-done.5
  139.0 0.8 select_bitcast_fusion.1
  139.9 0.0 all-reduce.8.cloned.1.call-update
  139.9 0.0 all-reduce.6.cloned.1.call-start
  139.9 0.0 copy-done.3
  139.9 0.2 copy.14
  140.2 0.0 copy-done.6
  140.2 9.8 %custom-call.3 = f32[1,128,128]{1,2,0:T(8,128)S(1)} custom-call(f32[1,128,128]{2,1,0:T(8,128)S(1)} %select_bitcast_fusion.3), custom_call_target="InvertDiagBlocksLowerTriangular" | custom-call | tf_op jit(solution)/shard_map/triangular_solve | solution.py:13
  150.0 204.8 %all-reduce.8.cloned.1.call-done = (f32[8,128,128]{1,2,0:T(8,128)}, f32[4,1,128,128]{3,2,0,1:T(8,128)}, f32[4,1,128,128]{3,2,0,1:T(8,128)}) async-done(((f32[8,128,128]{1,2,0:T(8,128)}, f32[4,1,128,128]{3,2,0,1:T(8,128)}, f32[4,1,128,128]{3,2,0,1:T(8,128)}), (f32[8,128,128]{1,2,0:T(8,128)}, f32[4,1,128,128]{3,2,0,1:T(8,128)}, f32[4,1,128,128]{3,2,0,1:T(8,128)})) %all-reduce.8.cloned.1.call-update) | async-done | bytes 1048592 | tf_op jit(solution)/shard_map/psum | solution.py:49
  354.8 0.0 copy-start.4
  354.8 1.1 pad_maximum_fusion
  355.9 0.2 copy.13
  356.1 0.0 copy-done.4
  356.1 0.1 fusion.10
  356.2 0.2 copy.15
  356.4 0.6 fusion.13
  357.0 0.0 copy-start.2
  357.0 1.6 convolution_negate_fusion
  358.7 0.0 all-reduce.6.cloned.1.call-update
  358.7 110.8 %all-reduce.6.cloned.1.call-done = f32[128,128]{1,0:T(8,128)} async-done(((f32[128,128]{1,0:T(8,128)}), f32[128,128]{1,0:T(8,128)}) %all-reduce.6.cloned.1.call-update) | async-done | bytes 65552 | tf_op jit(solution)/shard_map/psum | solution.py:55
  469.5 1.5 fusion.15
  471.0 0.0 copy-done.2
  (2 shorter events, 0.0 us)
Async XLA Ops:
  7.2 1.0 copy-start
  7.2 127.7 %all-reduce.10.cloned.1.call-start = ((), (), s32[]{:S(2)}) async-start(), calls=%async_computation.2 | async-start | bytes 1048576 | tf_op jit(solution)/shard_map/psum | solution.py:9
  8.4 126.5 %copy-start.1 = (f32[8,128,4,128]{3,2,1,0:T(4,128)S(1)}, f32[8,128,4,128]{3,2,1,0:T(4,128)}, u32[]{:S(2)}) copy-start(f32[8,128,4,128]{3,2,1,0:T(4,128)} %param.4) | copy-start | bytes 6291460
  15.0 339.8 %all-reduce.8.cloned.1.call-start = ((), (), s32[]{:S(2)}) async-start(), calls=%async_computation.1 | async-start | bytes 2097152 | tf_op jit(solution)/shard_map/psum | solution.py:49
  134.9 4.1 copy-start.5
  134.9 5.0 %copy-start.3 = (f32[8,128,128]{2,1,0:T(8,128)S(1)}, f32[8,128,128]{2,1,0:T(8,128)}, u32[]{:S(2)}) copy-start(f32[8,128,128]{2,1,0:T(8,128)} %param.6) | copy-start | bytes 1572868
  139.0 1.1 copy-start.6
  139.9 329.6 %all-reduce.6.cloned.1.call-start = ((), (), s32[]{:S(2)}) async-start(), calls=%async_computation | async-start | bytes 131072 | tf_op jit(solution)/shard_map/psum | solution.py:55
  354.8 1.3 copy-start.4
  357.0 114.0 %copy-start.2 = (f32[1024,128]{1,0:T(8,128)}, f32[1024,128]{1,0:T(8,128)S(1)}, u32[]{:S(2)}) copy-start(f32[1024,128]{1,0:T(8,128)S(1)} %fusion.13) | copy-start | bytes 1572868
Sparse Core Ops, SparseCore 0:
  15.1 119.7 all-reduce.9
  140.0 214.7 all-reduce.7
  358.8 110.6 all-reduce.5
where the time goes:
time: 478 us
  waiting for transfers between devices  436 us (91%)
  other arithmetic  14.1 us (3%)
  between operations  13.9 us (3%)
  matrix products  12.2 us (3%)
    psum x1, waiting for transfers between devices, per_device(): direct = lax.psum(direct_part, 'col').reshape(row_blocks * width, width)  205 us
    psum x1, waiting for transfers between devices, spread(): return lax.psum(jnp.where(mine, value, jnp.zeros_like(value)), axis)  120 us
    psum x1, waiting for transfers between devices, per_device(): gram = lax.psum(gram_part, 'row')  111 us
    another operation x2, other arithmetic, solve_rows(): lax.linalg.triangular_solve(diag_block, total, left_side=False, lower=True)  9.82 us
  transfers between devices with their start and end apart: 3, of which 3 were waited for; matrix products, arithmetic and copies ran while one was open for 2% of the time, Pallas kernels for 0%

commit v1 on v0

v1 whole, which is shorter than its diff:
```python
import functools

import jax
import jax.numpy as jnp
from jax import lax
from jax.experimental import pallas as pl
from jax.experimental.pallas import tpu as pltpu
from jax.sharding import PartitionSpec as P

MESH = pl.DeviceIdType.MESH
F32 = jnp.float32
HI = lax.Precision.HIGHEST
BLK = 128


def dot(a, b):
    return jnp.dot(a, b, precision=HI, preferred_element_type=F32)


def dot_t(a, b):
    return lax.dot_general(
        a, b, (((0,), (0,)), ((), ())), precision=HI, preferred_element_type=F32
    )


def invert_lower(d):
    n = d.shape[0]
    row = lax.broadcasted_iota(jnp.int32, (n, n), 0)
    col = lax.broadcasted_iota(jnp.int32, (n, n), 1)
    eye = row == col
    zero = jnp.zeros_like(d)
    diag = jnp.where(eye, d, zero)
    recip_row = 1.0 / jnp.sum(diag, axis=1, keepdims=True)
    recip_col = 1.0 / jnp.sum(diag, axis=0, keepdims=True)

    def below(shift):
        same = lax.shift_right_logical(row, shift + 1) == lax.shift_right_logical(col, shift + 1)
        other = lax.shift_right_logical(row, shift) != lax.shift_right_logical(col, shift)
        return jnp.where(same & other & (row > col), d, zero)

    inv = jnp.where(eye, jnp.broadcast_to(recip_row, (n, n)), -(below(0) * recip_row) * recip_col)
    shift = 1
    while (1 << shift) < n:
        inv = inv - dot(inv, dot(below(shift), inv))
        shift += 1
    return inv


def kernel(
    rows,
    cols,
    s_hbm,
    panel_hbm,
    given_hbm,
    diag_hbm,
    x_out,
    g_out,
    s_v,
    p_v,
    b_v,
    d_v,
    pt_v,
    inv_v,
    lc,
    flip_v,
    flip_in,
    route_src,
    route_in,
    half_v,
    give_v,
    pair_in,
    agg_far,
    agg_near,
    agg_out,
    fin_in,
    x_v,
    prod_v,
    prod_in,
    psum_v,
    psum_in,
    ppair_v,
    ppair_in,
    pfull_v,
    gram_v,
    loc,
    sc_s,
    sc_r,
    ag_s,
    ag_r,
    fl_s,
    fl_r,
    rt_s,
    rt_r,
    pr_s,
    pr_r,
    rs_s,
    rs_r,
    x_s,
    x_r,
    xp_s,
    xp_r,
    g_s,
    g_r,
):
    R, C = rows, cols
    Z = C // 2
    W = Z // 4
    SL = 8 * BLK // C
    NS = BLK // SL
    HALF = 4 * NS
    r = lax.axis_index("row")
    c = lax.axis_index("col")
    z = c // 2
    k = c % 2

    def dev(row, chip, core):
        return (row, chip * 2 + core)

    def copy(src, dst, send, recv, device):
        return pltpu.make_async_remote_copy(
            src_ref=src,
            dst_ref=dst,
            send_sem=send,
            recv_sem=recv,
            device_id=device,
            device_id_type=MESH,
        )

    def wait(ref, sem):
        pltpu.make_async_copy(ref, ref, sem).wait()

    def offset_of(row, chip):
        return (chip - row // 2 + R // 4 + Z) % Z

    def slice_in_half(o):
        m = o % (R // 2)
        return (2 * (m // NS) + o // (R // 2)) * NS + m % NS

    cp_panel = pltpu.make_async_copy(panel_hbm, p_v, loc.at[0])
    cp_panel.start()
    cp_s = []
    for a in range(8):
        cp_s.append(pltpu.make_async_copy(s_hbm.at[a], s_v.at[a], loc.at[1 + a]))
        cp_s[a].start()
    my_slice = slice_in_half(offset_of(r, z))
    sid = k * HALF + my_slice
    cp_b = pltpu.make_async_copy(given_hbm.at[sid], b_v, loc.at[9])
    cp_b.start()
    cp_d = pltpu.make_async_copy(diag_hbm, d_v, loc.at[10])
    cp_d.start()

    to_r = c % R
    to_z = (z - R // 4 + r % (R // 2) + Z) % Z
    to_k = r // (R // 2)
    to_self = (to_r == r) & (to_z == z) & (to_k == k)
    off = offset_of(r, z)
    from_r = k * (R // 2) + off % (R // 2)
    from_c = r + R * (off // (R // 2))

    barrier = pltpu.get_barrier_semaphore()
    for i in range(1, R):
        pl.semaphore_signal(barrier, inc=1, device_id=((r + i) % R, c), device_id_type=MESH)
    for i in range(1, Z):
        pl.semaphore_signal(barrier, inc=1, device_id=dev(r, (z + i) % Z, k), device_id_type=MESH)
    pl.semaphore_signal(barrier, inc=1, device_id=dev(r, z, 1 - k), device_id_type=MESH)
    pl.semaphore_signal(barrier, inc=1, device_id=(from_r, from_c), device_id_type=MESH)
    pl.semaphore_wait(barrier, R - 1 + Z - 1 + 2)

    owner = c % R
    which = c // R
    own = owner == r

    def piece(s):
        return panel_hbm.at[(2 * (s // NS) + which) * NS + s % NS]

    @pl.when(own)
    def _():
        for i in range(1, R):
            s = (r + i) % R
            copy(piece(s), lc.at[s], sc_s, sc_r, (s, c)).start()
        mine = pltpu.make_async_copy(piece(r), lc.at[r], loc.at[11])
        mine.start()
        mine.wait()

    cp_panel.wait()
    for a in range(8):
        block = p_v[pl.ds(a * NS, NS)].reshape(BLK, BLK)
        pt_v[:, pl.ds(a * BLK, BLK)] = block.T
    for a in range(8):
        cp_s[a].wait()
    for b in range(4):
        tall = jnp.concatenate([s_v[a, pl.ds(b, BLK, stride=4), :] for a in range(8)], axis=0)
        part = dot(pt_v[...], tall)
        flip_v[pl.ds(b * NS, NS)] = part.T.reshape(NS, SL, BLK)
    for i in range(1, R):
        s = (r + i) % R
        copy(flip_v.at[s], flip_in.at[r], fl_s, fl_r, (s, c)).start()

    @pl.when(jnp.logical_not(own))
    def _():
        wait(lc.at[r], sc_r)

    for i in range(1, R):
        s = (r + i) % R
        copy(lc.at[r], lc.at[r], ag_s, ag_r, (s, c)).start()

    cp_d.wait()
    inv_v[...] = invert_lower(d_v[...])

    wait(flip_in.at[pl.ds(0, R - 1)], fl_r)
    flip_in[r] = flip_v[r]
    total_flip = flip_in[0]
    for i in range(1, R):
        total_flip = total_flip + flip_in[i]
    route_src[...] = total_flip

    @pl.when(jnp.logical_not(to_self))
    def _():
        copy(route_src, route_in, rt_s, rt_r, dev(to_r, to_z, to_k)).start()

    wait(lc.at[pl.ds(0, R - 1)], ag_r)
    weights = lc[...].reshape(4 * BLK, BLK)

    def direct_half(base):
        stacked = jnp.concatenate(
            [
                jnp.concatenate(
                    [s_v[base + a, pl.ds(b, BLK, stride=4), :] for b in range(4)], axis=1
                )
                for a in range(4)
            ],
            axis=0,
        )
        return dot(stacked, weights).reshape(HALF, SL, BLK)

    give_v[...] = direct_half((1 - k) * 4)
    pair = copy(give_v, pair_in, pr_s, pr_r, dev(r, z, 1 - k))
    pair.start()
    half_v[...] = direct_half(k * 4)
    own_sum = dot(
        pt_v[:, pl.ds(pl.multiple_of(k * 4 * BLK, BLK), 4 * BLK)], half_v[...].reshape(4 * BLK, BLK)
    ) + dot(
        pt_v[:, pl.ds(pl.multiple_of((1 - k) * 4 * BLK, BLK), 4 * BLK)],
        give_v[...].reshape(4 * BLK, BLK),
    )
    pair.wait()
    half_v[...] = half_v[...] + pair_in[...]

    def slice_for(delta):
        return slice_in_half(offset_of(r, (z + delta + Z) % Z))

    def chip(delta):
        return dev(r, (z + delta + Z) % Z, k)

    for d in range(2 * W, W, -1):
        copy(half_v.at[slice_for(d)], agg_far.at[d - W - 1], rs_s, rs_r.at[0], chip(d - W)).start()
    for d in range(2 * W - 1, W, -1):
        copy(half_v.at[slice_for(-d)], agg_near.at[d - W - 1], rs_s, rs_r.at[1], chip(W - d)).start()
    for d in range(W - 1, 0, -1):
        copy(half_v.at[slice_for(d)], fin_in.at[d - 1], rs_s, rs_r.at[2], chip(d)).start()
        copy(half_v.at[slice_for(-d)], fin_in.at[W - 1 + d - 1], rs_s, rs_r.at[2], chip(-d)).start()

    cp_b.wait()
    prod = dot_t(b_v[...], p_v[sid]) - own_sum - own_sum.T
    GL = BLK // R
    prod_v[...] = prod.reshape(R, GL, BLK)
    for i in range(1, R):
        s = (r + i) % R
        copy(prod_v.at[s], prod_in.at[r], g_s.at[0], g_r.at[0], (s, c)).start()

    wait(agg_far, rs_r.at[0])
    far = half_v[slice_for(W)]
    for i in range(W):
        far = far + agg_far[i]
    agg_out[0] = far
    copy(agg_out.at[0], fin_in.at[2 * W - 2], rs_s, rs_r.at[2], chip(W)).start()
    near = half_v[slice_for(-W)]
    if W > 1:
        wait(agg_near.at[pl.ds(0, W - 1)], rs_r.at[1])
        for i in range(W - 1):
            near = near + agg_near[i]
    agg_out[1] = near
    copy(agg_out.at[1], fin_in.at[2 * W - 1], rs_s, rs_r.at[2], chip(-W)).start()

    wait(prod_in.at[pl.ds(0, R - 1)], g_r.at[0])
    prod_in[r] = prod_v[r]
    acc = prod_in[0]
    for i in range(1, R):
        acc = acc + prod_in[i]
    psum_v[...] = acc
    for i in range(1, Z):
        copy(psum_v, psum_in.at[z], g_s.at[1], g_r.at[1], chip(i)).start()

    @pl.when(jnp.logical_not(to_self))
    def _():
        wait(route_in, rt_r)

    @pl.when(to_self)
    def _():
        route_in[...] = route_src[...]

    wait(fin_in, rs_r.at[2])
    total = half_v[my_slice]
    for i in range(2 * W):
        total = total + fin_in[i]
    total = b_v[...] - (total + route_in[...])
    x_v[sid] = dot(total, inv_v[...])

    def sid_at(delta):
        return k * HALF + slice_for(delta)

    def forward(s):
        copy(x_v.at[s], x_v.at[s], xp_s, xp_r, dev(r, z, 1 - k)).start()

    for d in range(W, 0, -1):
        copy(x_v.at[sid], x_v.at[sid], x_s, x_r.at[d], chip(d)).start()
        copy(x_v.at[sid], x_v.at[sid], x_s, x_r.at[2 * W + d], chip(-d)).start()
    forward(sid)
    far_sid = sid_at(-W)
    wait(x_v.at[far_sid], x_r.at[W])
    for d in range(W, 0, -1):
        copy(x_v.at[far_sid], x_v.at[far_sid], x_s, x_r.at[W + d], chip(d)).start()
    near_sid = sid_at(W)
    wait(x_v.at[near_sid], x_r.at[3 * W])
    for d in range(W - 1, 0, -1):
        copy(x_v.at[near_sid], x_v.at[near_sid], x_s, x_r.at[3 * W + d], chip(-d)).start()
    forward(far_sid)
    forward(near_sid)
    for d in range(1, W):
        wait(x_v.at[sid_at(-d)], x_r.at[d])
        forward(sid_at(-d))
        wait(x_v.at[sid_at(d)], x_r.at[2 * W + d])
        forward(sid_at(d))

    wait(psum_in.at[pl.ds(0, Z - 1)], g_r.at[1])
    psum_in[z] = psum_v[...]
    acc = psum_in[0]
    for i in range(1, Z):
        acc = acc + psum_in[i]
    ppair_v[...] = acc
    hand = copy(ppair_v, ppair_in, g_s.at[2], g_r.at[2], dev(r, z, 1 - k))
    hand.start()
    hand.wait()
    pfull_v[r] = ppair_v[...] + ppair_in[...]
    for i in range(1, R):
        copy(pfull_v.at[r], pfull_v.at[r], g_s.at[3], g_r.at[3], ((r + i) % R, c)).start()

    for d in range(1, W):
        wait(x_v.at[sid_at(-W - d)], x_r.at[W + d])
        forward(sid_at(-W - d))
        wait(x_v.at[sid_at(W + d)], x_r.at[3 * W + d])
        forward(sid_at(W + d))
    wait(x_v.at[sid_at(-2 * W)], x_r.at[2 * W])
    forward(sid_at(-2 * W))

    wait(pfull_v.at[pl.ds(0, R - 1)], g_r.at[3])
    full = pfull_v[...].reshape(BLK, BLK)
    gram = -dot_t(inv_v[...], full)
    row = lax.broadcasted_iota(jnp.int32, (BLK, BLK), 0)
    col = lax.broadcasted_iota(jnp.int32, (BLK, BLK), 1)
    gram_v[...] = jnp.where(row >= col, gram, jnp.zeros_like(gram))
    out_g = pltpu.make_async_copy(gram_v, g_out, loc.at[13])
    out_g.start()

    wait(x_v.at[pl.ds(0, HALF)], xp_r)
    out_x = pltpu.make_async_copy(x_v, x_out, loc.at[12])
    out_x.start()

    @pl.when(own)
    def _():
        wait(lc.at[pl.ds(0, R - 1)], sc_s)

    wait(lc.at[pl.ds(0, R - 1)], ag_s)
    wait(flip_in.at[pl.ds(0, R - 1)], fl_s)

    @pl.when(jnp.logical_not(to_self))
    def _():
        wait(route_src, rt_s)

    wait(half_v.at[pl.ds(0, Z - 1)], rs_s)
    wait(half_v.at[pl.ds(0, Z - 1)], x_s)
    wait(half_v, xp_s)
    wait(prod_in.at[pl.ds(0, R - 1)], g_s.at[0])
    wait(psum_in.at[pl.ds(0, Z - 1)], g_s.at[1])
    wait(pfull_v.at[pl.ds(0, R - 1)], g_s.at[3])
    out_g.wait()
    out_x.wait()


def solution(mesh):
    R, C = mesh.shape["row"], mesh.shape["col"]
    Z = C // 2
    W = Z // 4
    SL = 8 * BLK // C
    NS = BLK // SL
    HALF = 4 * NS
    GL = BLK // R

    def per_device(trail_adjoint, panel, panel_adjoint, diag_block):
        any_spec = pl.BlockSpec(memory_space=pl.ANY)
        vm = lambda *shape: pltpu.VMEM(shape, F32)
        dma = pltpu.SemaphoreType.DMA
        x, gram = pl.pallas_call(
            functools.partial(kernel, R, C),
            out_shape=(
                jax.ShapeDtypeStruct((2 * HALF, SL, BLK), F32),
                jax.ShapeDtypeStruct((BLK, BLK), F32),
            ),
            in_specs=[any_spec] * 4,
            out_specs=(any_spec, any_spec),
            scratch_shapes=[
                vm(8, 4 * BLK, BLK),
                vm(2 * HALF, SL, BLK),
                vm(SL, BLK),
                vm(BLK, BLK),
                vm(BLK, 8 * BLK),
                vm(BLK, BLK),
                vm(R, SL, BLK),
                vm(R, SL, BLK),
                vm(R, SL, BLK),
                vm(SL, BLK),
                vm(SL, BLK),
                vm(HALF, SL, BLK),
                vm(HALF, SL, BLK),
                vm(HALF, SL, BLK),
                vm(W, SL, BLK),
                vm(max(W - 1, 1), SL, BLK),
                vm(2, SL, BLK),
                vm(2 * W, SL, BLK),
                vm(2 * HALF, SL, BLK),
                vm(R, GL, BLK),
                vm(R, GL, BLK),
                vm(GL, BLK),
                vm(Z, GL, BLK),
                vm(GL, BLK),
                vm(GL, BLK),
                vm(R, GL, BLK),
                vm(BLK, BLK),
                dma((14,)),
                dma(()),
                dma(()),
                dma(()),
                dma(()),
                dma(()),
                dma(()),
                dma(()),
                dma(()),
                dma(()),
                dma(()),
                dma(()),
                dma((3,)),
                dma(()),
                dma((4 * W + 1,)),
                dma(()),
                dma(()),
                dma((4,)),
                dma((4,)),
            ],
            compiler_params=pltpu.CompilerParams(
                collective_id=0, has_side_effects=True, vmem_limit_bytes=32 * 1024 * 1024
            ),
        )(
            trail_adjoint.reshape(8, 4 * BLK, BLK),
            panel.reshape(2 * HALF, SL, BLK),
            panel_adjoint.reshape(2 * HALF, SL, BLK),
            diag_block,
        )
        return x.reshape(8, BLK, BLK), gram

    return jax.shard_map(
        per_device,
        mesh=mesh,
        in_specs=(P(None, "row", None, "col"), P(None, "row", None), P(None, "row", None), P()),
        out_specs=(P(None, "row", None), P()),
        check_vma=False,
    )
```

time: 478 us -> 64.6 us (0.14)
  waiting for transfers between devices: 436 us -> 0 us
  Pallas kernels: 0 us -> 57.8 us
  other arithmetic: 14.1 us -> 0 us
  between operations: 13.9 us -> 0.65 us
  matrix products: 12.2 us -> 0 us
    psum x3 -> x0, waiting for transfers between devices: 435 us -> none  [the longest x1 205 us: per_device(): direct = lax.psum(direct_part, 'col').reshape(row_blocks * width, width)]
    pallas_call x0 -> x1, Pallas kernels: none -> 57.8 us  [per_device(): pl.pallas_call(functools.partial(kernel, R, C), out_shape=(jax.ShapeDtype...]
    another operation x4 -> x0, other arithmetic: 11.8 us -> none  [the longest x2 9.82 us: solve_rows(): lax.linalg.triangular_solve(diag_block, total, left_side=False, lower=True)]
    dot_general x3 -> x0, matrix products: 11.6 us -> none  [the longest x1 5.85 us: per_device(): jnp.einsum('aibj,aik->bjk', trail_adjoint, panel, precision=lax.Precision...]
  transfers between devices with their start and end apart: 3 -> 0, of which waited for: 3 -> 0; matrix products, arithmetic and copies ran while one was open for 2% -> 0% of each run, Pallas kernels for 0% -> 0%
where the time goes in v1:
time: 64.6 us; the launch traced here: 64.3 us
  Pallas kernels  57.8 us (89%)
  local copies, waits for them, and re-layouts  5.93 us (9%)
  between operations  0.65 us (1%)
    pallas_call x1, Pallas kernels, per_device(): pl.pallas_call(functools.partial(kernel, R, C), out_shape=(jax.ShapeDtype...  57.8 us
    unnamed x10, local copies, waits for them, and re-layouts  5.93 us

profile of v1, /device:TPU:1, one launch (start us, length us, event | category | flops | bytes accessed | tf_op | source)
XLA Modules:
  0.0 64.3 jit_solution(15061647993336575716)
XLA Ops:
  0.6 0.0 copy-start
  0.6 1.6 %copy-done = f32[8,128,4,128]{3,2,1,0:T(4,128)S(1)} copy-done((f32[8,128,4,128]{3,2,1,0:T(4,128)S(1)}, f32[8,128,4,128]{3,2,1,0:T(4,128)}, u32[]{:S(2)}) %copy-start) | copy-done | bytes 2097176
  2.2 0.0 copy-start.1
  2.2 1.0 %copy-done.1 = f32[8,128,128]{2,1,0:T(8,128)S(1)} copy-done((f32[8,128,128]{2,1,0:T(8,128)S(1)}, f32[8,128,128]{2,1,0:T(8,128)}, u32[]{:S(2)}) %copy-start.1) | copy-done | bytes 524312
  3.3 0.0 copy-start.2
  3.3 1.0 %copy-done.2 = f32[8,128,128]{2,1,0:T(8,128)S(1)} copy-done((f32[8,128,128]{2,1,0:T(8,128)S(1)}, f32[8,128,128]{2,1,0:T(8,128)}, u32[]{:S(2)}) %copy-start.2) | copy-done | bytes 524312
  4.3 0.0 copy-start.3
  4.3 0.8 %copy-done.3 = f32[128,128]{1,0:T(8,128)S(1)} copy-done((f32[128,128]{1,0:T(8,128)S(1)}, f32[128,128]{1,0:T(8,128)}, u32[]{:S(2)}) %copy-start.3) | copy-done | bytes 65560
  5.1 57.8 %shard_map.59 = (f32[32,32,128]{2,1,0:T(8,128)S(1)}, f32[128,128]{1,0:T(8,128)S(1)}) custom-call(f32[8,512,128]{2,1,0:T(8,128)S(1)} %bitcast.4, f32[32,32,128]{2,1,0:T(8,128)S(1)} %bitcast.5, f32[32,32,128]{2,1,0:T(8,128)S(1)} %bitcast.6, f32[128,128]{1,0:T(8,128)S(1)} %copy-done.3), custom_call_target="tpu_custom_call" | custom-call | tf_op jit(solution)/shard_map/pallas_call | solution.py:403
  62.9 0.8 %copy.8 = f32[8,128,128]{2,1,0:T(8,128)} copy(f32[8,128,128]{2,1,0:T(8,128)S(1)} %bitcast.7) | data formatting | bytes 1048576
  63.7 0.6 copy.9
Async XLA Ops:
  0.6 1.6 %copy-start = (f32[8,128,4,128]{3,2,1,0:T(4,128)S(1)}, f32[8,128,4,128]{3,2,1,0:T(4,128)}, u32[]{:S(2)}) copy-start(f32[8,128,4,128]{3,2,1,0:T(4,128)} %param.4) | copy-start | bytes 6291460
  2.2 1.0 %copy-start.1 = (f32[8,128,128]{2,1,0:T(8,128)S(1)}, f32[8,128,128]{2,1,0:T(8,128)}, u32[]{:S(2)}) copy-start(f32[8,128,128]{2,1,0:T(8,128)} %param.5) | copy-start | bytes 1572868
  3.3 1.0 %copy-start.2 = (f32[8,128,128]{2,1,0:T(8,128)S(1)}, f32[8,128,128]{2,1,0:T(8,128)}, u32[]{:S(2)}) copy-start(f32[8,128,128]{2,1,0:T(8,128)} %param.6) | copy-start | bytes 1572868
  4.3 0.8 %copy-start.3 = (f32[128,128]{1,0:T(8,128)S(1)}, f32[128,128]{1,0:T(8,128)}, u32[]{:S(2)}) copy-start(f32[128,128]{1,0:T(8,128)} %diag_hbm.1) | copy-start | bytes 196612

commit v2 on v1

v2 whole, which is shorter than its diff:
```python
import functools

import jax
import jax.numpy as jnp
from jax import lax
from jax.experimental import pallas as pl
from jax.experimental.pallas import tpu as pltpu
from jax.sharding import PartitionSpec as P

MESH = pl.DeviceIdType.MESH
F32 = jnp.float32
BF16 = jnp.bfloat16
HI = lax.Precision.HIGHEST
BLK = 128


def dot(a, b):
    return jnp.dot(a, b, precision=HI, preferred_element_type=F32)


def dot_t(a, b):
    return lax.dot_general(
        a, b, (((0,), (0,)), ((), ())), precision=HI, preferred_element_type=F32
    )


def invert_lower(d):
    n = d.shape[0]
    row = lax.broadcasted_iota(jnp.int32, (n, n), 0)
    col = lax.broadcasted_iota(jnp.int32, (n, n), 1)
    eye = row == col
    zero = jnp.zeros_like(d)
    diag = jnp.where(eye, d, zero)
    recip_row = 1.0 / jnp.sum(diag, axis=1, keepdims=True)
    recip_col = 1.0 / jnp.sum(diag, axis=0, keepdims=True)

    def below(shift):
        same = lax.shift_right_logical(row, shift + 1) == lax.shift_right_logical(col, shift + 1)
        other = lax.shift_right_logical(row, shift) != lax.shift_right_logical(col, shift)
        return jnp.where(same & other & (row > col), d, zero)

    inv = jnp.where(eye, jnp.broadcast_to(recip_row, (n, n)), -(below(0) * recip_row) * recip_col)
    shift = 1
    while (1 << shift) < n:
        inv = inv - dot(inv, dot(below(shift), inv))
        shift += 1
    return inv


def split(x):
    hi = x.astype(BF16)
    return hi, (x - hi.astype(F32)).astype(BF16)


def bdot(a, b):
    return jnp.dot(a, b, preferred_element_type=F32)


def kernel(
    rows,
    cols,
    s_hbm,
    panel_hbm,
    given_hbm,
    diag_hbm,
    x_v,
    g_out,
    s_v,
    s_hi,
    s_lo,
    p_v,
    b_v,
    d_v,
    pt_v,
    inv_v,
    lc,
    flip_v,
    flip_in,
    route_src,
    route_in,
    half_v,
    give_v,
    pair_in,
    agg_far,
    agg_near,
    agg_out,
    fin_in,
    prod_v,
    prod_in,
    quad_v,
    quad_in,
    cross_v,
    cross_in,
    ppair_v,
    ppair_in,
    pfull_v,
    loc,
    sc_s,
    sc_r,
    ag_s,
    ag_r,
    fl_s,
    fl_r,
    rt_s,
    rt_r,
    pr_s,
    pr_r,
    rs_s,
    rs_r,
    x_s,
    x_r,
    xp_s,
    xp_r,
    g_s,
    g_r,
):
    R, C = rows, cols
    Z = C // 2
    W = Z // 4
    SL = 8 * BLK // C
    NS = BLK // SL
    HALF = 4 * NS
    HR = 4 * BLK
    r = lax.axis_index("row")
    c = lax.axis_index("col")
    z = c // 2
    k = c % 2

    def dev(row, chip, core):
        return (row, chip * 2 + core)

    def plane(i):
        return ((r + i) & (R - 1), c)

    def chip(delta):
        return dev(r, (z + delta) & (Z - 1), k)

    def copy(src, dst, send, recv, device):
        return pltpu.make_async_remote_copy(
            src_ref=src,
            dst_ref=dst,
            send_sem=send,
            recv_sem=recv,
            device_id=device,
            device_id_type=MESH,
        )

    def wait(ref, sem):
        pltpu.make_async_copy(ref, ref, sem).wait()

    def offset_of(row, at):
        return (at - row // 2 + R // 4) & (Z - 1)

    def slice_in_half(o):
        m = o & (R // 2 - 1)
        return (2 * (m // NS) + o // (R // 2)) * NS + (m & (NS - 1))

    def slice_for(delta):
        return slice_in_half(offset_of(r, (z + delta) & (Z - 1)))

    barrier = pltpu.get_barrier_semaphore()
    other = dev(r, z, 1 - k)
    for i in range(1, R):
        pl.semaphore_signal(barrier, inc=1, device_id=plane(i), device_id_type=MESH)
    for i in range(1, W + 1):
        for delta in (i, -i):
            for core in (0, 1):
                near_by = dev(r, (z + delta) & (Z - 1), core)
                pl.semaphore_signal(barrier, inc=1, device_id=near_by, device_id_type=MESH)
    pl.semaphore_signal(barrier, inc=1, device_id=other, device_id_type=MESH)

    cp_s = [pltpu.make_async_copy(s_hbm.at[a], s_v.at[a], loc.at[1 + a]) for a in range(8)]
    cp_panel = pltpu.make_async_copy(panel_hbm, p_v, loc.at[0])
    for one in cp_s:
        one.start()
    cp_panel.start()
    my_slice = slice_for(0)
    sid = k * HALF + my_slice
    cp_b = pltpu.make_async_copy(given_hbm.at[sid], b_v, loc.at[9])
    cp_b.start()
    cp_d = pltpu.make_async_copy(diag_hbm, d_v, loc.at[10])
    cp_d.start()

    pl.semaphore_wait(barrier, R - 1 + 4 * W + 1)

    owner = c & (R - 1)
    which = c // R
    own = owner == r

    def piece(s):
        return panel_hbm.at[(2 * (s // NS) + which) * NS + (s & (NS - 1))]

    @pl.when(own)
    def _():
        for i in range(1, R):
            s = (r + i) & (R - 1)
            copy(piece(s), lc.at[s], sc_s, sc_r, plane(i)).start()
        mine = pltpu.make_async_copy(piece(r), lc.at[r], loc.at[11])
        mine.start()
        mine.wait()

    for a in range(8):
        cp_s[a].wait()

        for b in range(4):
            hi, lo = split(s_v[a, pl.ds(b, BLK, stride=4), :])
            s_hi[pl.ds(a * BLK, BLK), pl.ds(b * BLK, BLK)] = hi
            s_lo[pl.ds(a * BLK, BLK), pl.ds(b * BLK, BLK)] = lo
    cp_panel.wait()
    for a in range(8):
        hi, lo = split(p_v[pl.ds(a * NS, NS)].reshape(BLK, BLK).T)
        pt_v[pl.ds(0, BLK), pl.ds(a * BLK, BLK)] = hi
        pt_v[pl.ds(BLK, BLK), pl.ds(a * BLK, BLK)] = lo
    for b in range(2):
        wide = pl.ds(b * 2 * BLK, 2 * BLK)
        both = bdot(pt_v[...], s_hi[:, wide])
        part = both[:BLK] + (both[BLK:] + bdot(pt_v[pl.ds(0, BLK), :], s_lo[:, wide]))
        flip_v[pl.ds(b * 2 * NS, 2 * NS)] = part.T.reshape(2 * NS, SL, BLK)
    for i in range(1, R):
        copy(flip_v.at[(r + i) & (R - 1)], flip_in.at[r], fl_s, fl_r, plane(i)).start()

    @pl.when(jnp.logical_not(own))
    def _():
        wait(lc.at[r], sc_r)

    for i in range(1, R):
        copy(lc.at[r], lc.at[r], ag_s, ag_r, plane(i)).start()

    cp_d.wait()
    inv_v[...] = invert_lower(d_v[...])

    wait(flip_in.at[pl.ds(0, R - 1)], fl_r)
    flip_in[r] = flip_v[r]
    total_flip = flip_in[0]
    for i in range(1, R):
        total_flip = total_flip + flip_in[i]
    route_src[...] = total_flip

    wait(lc.at[pl.ds(0, R - 1)], ag_r)

    to_r = owner
    to_z = (z - R // 4 + (r & (R // 2 - 1))) & (Z - 1)
    to_k = r // (R // 2)
    to_self = (to_r == r) & (to_z == z) & (to_k == k)

    @pl.when(jnp.logical_not(to_self))
    def _():
        copy(route_src, route_in, rt_s, rt_r, dev(to_r, to_z, to_k)).start()

    @pl.when(to_self)
    def _():
        route_in[...] = route_src[...]

    w_hi, w_lo = split(lc[...].reshape(HR, BLK))
    w_both = jnp.concatenate([w_hi, w_lo], axis=1)

    def direct_half(base):
        at = pl.ds(pl.multiple_of(base * HR, HR), HR)
        both = bdot(s_hi[at, :], w_both)
        out = both[:, :BLK] + (both[:, BLK:] + bdot(s_lo[at, :], w_hi))
        return out.reshape(HALF, SL, BLK)

    give_v[...] = direct_half(1 - k)
    pair = copy(give_v, pair_in, pr_s, pr_r, other)
    pair.start()
    kept = direct_half(k)
    kept_hi, kept_lo = split(kept.reshape(HR, BLK))
    pair.wait()
    half_v[...] = kept + pair_in[...]

    for d in range(2 * W, W, -1):
        copy(half_v.at[slice_for(d)], agg_far.at[d - W - 1], rs_s, rs_r.at[0], chip(d - W)).start()
        if d < 2 * W:
            copy(
                half_v.at[slice_for(-d)], agg_near.at[d - W - 1], rs_s, rs_r.at[1], chip(W - d)
            ).start()
    for d in range(W - 1, 0, -1):
        copy(half_v.at[slice_for(d)], fin_in.at[d - 1], rs_s, rs_r.at[2], chip(d)).start()
        copy(half_v.at[slice_for(-d)], fin_in.at[W + d - 2], rs_s, rs_r.at[2], chip(-d)).start()

    def product(base, hi, lo):
        at = pl.ds(pl.multiple_of(base * HR, HR), HR)
        both = bdot(pt_v[:, at], hi)
        return both[:BLK] + (both[BLK:] + bdot(pt_v[pl.ds(0, BLK), at], lo))

    give_hi, give_lo = split(give_v[...].reshape(HR, BLK))
    own_sum = product(k, kept_hi, kept_lo) + product(1 - k, give_hi, give_lo)
    cp_b.wait()
    prod = dot_t(b_v[...], p_v[sid]) - (own_sum + own_sum.T)
    prod_v[...] = prod.reshape(R, BLK // R, BLK)
    for i in range(1, R):
        copy(prod_v.at[(r + i) & (R - 1)], prod_in.at[r], g_s.at[0], g_r.at[0], plane(i)).start()

    wait(agg_far, rs_r.at[0])
    far = half_v[slice_for(W)]
    for i in range(W):
        far = far + agg_far[i]
    agg_out[0] = far
    copy(agg_out.at[0], fin_in.at[2 * W - 2], rs_s, rs_r.at[2], chip(W)).start()
    near = half_v[slice_for(-W)]
    if W > 1:
        wait(agg_near.at[pl.ds(0, W - 1)], rs_r.at[1])
        for i in range(W - 1):
            near = near + agg_near[i]
    agg_out[1] = near
    copy(agg_out.at[1], fin_in.at[2 * W - 1], rs_s, rs_r.at[2], chip(-W)).start()

    wait(prod_in.at[pl.ds(0, R - 1)], g_r.at[0])
    prod_in[r] = prod_v[r]
    acc = prod_in[0]
    for i in range(1, R):
        acc = acc + prod_in[i]
    group, lane = z // W, z & (W - 1)
    quad_v[...] = acc
    for i in range(1, W):
        mate = dev(r, group * W + ((lane + i) & (W - 1)), k)
        copy(quad_v, quad_in.at[lane], g_s.at[1], g_r.at[1], mate).start()

    @pl.when(jnp.logical_not(to_self))
    def _():
        wait(route_in, rt_r)

    wait(fin_in, rs_r.at[2])
    total = half_v[my_slice]
    for i in range(2 * W):
        total = total + fin_in[i]
    total = b_v[...] - (total + route_in[...])
    x_v[sid] = dot(total, inv_v[...])

    def sid_at(delta):
        return k * HALF + slice_for(delta)

    def send_x(s, sem, device):
        copy(x_v.at[s], x_v.at[s], x_s, x_r.at[sem], device).start()

    def forward(s):
        copy(x_v.at[s], x_v.at[s], xp_s, xp_r, other).start()

    for d in range(W, 0, -1):
        send_x(sid, d, chip(d))
        send_x(sid, 2 * W + d, chip(-d))
    forward(sid)

    if W > 1:
        wait(quad_in.at[pl.ds(0, W - 1)], g_r.at[1])
    quad_in[lane] = quad_v[...]
    acc = quad_in[0]
    for i in range(1, W):
        acc = acc + quad_in[i]
    cross_v[...] = acc
    for i in range(1, 4):
        copy(cross_v, cross_in.at[group], g_s.at[2], g_r.at[2], chip(i * W)).start()

    far_sid = sid_at(-W)
    wait(x_v.at[far_sid], x_r.at[W])
    for d in range(W, 0, -1):
        send_x(far_sid, W + d, chip(d))
    near_sid = sid_at(W)
    wait(x_v.at[near_sid], x_r.at[3 * W])
    for d in range(W - 1, 0, -1):
        send_x(near_sid, 3 * W + d, chip(-d))
    forward(far_sid)
    forward(near_sid)
    for d in range(1, W):
        wait(x_v.at[sid_at(-d)], x_r.at[d])
        forward(sid_at(-d))
        wait(x_v.at[sid_at(d)], x_r.at[2 * W + d])
        forward(sid_at(d))

    wait(cross_in.at[pl.ds(0, 3)], g_r.at[2])
    cross_in[group] = cross_v[...]
    ppair_v[...] = (cross_in[0] + cross_in[1]) + (cross_in[2] + cross_in[3])
    hand = copy(ppair_v, ppair_in, g_s.at[3], g_r.at[3], other)
    hand.start()
    hand.wait()
    pfull_v[r] = ppair_v[...] + ppair_in[...]
    for i in range(1, R):
        copy(pfull_v.at[r], pfull_v.at[r], g_s.at[4], g_r.at[4], plane(i)).start()

    for d in range(1, W):
        wait(x_v.at[sid_at(-W - d)], x_r.at[W + d])
        forward(sid_at(-W - d))
        wait(x_v.at[sid_at(W + d)], x_r.at[3 * W + d])
        forward(sid_at(W + d))
    wait(x_v.at[sid_at(-2 * W)], x_r.at[2 * W])
    forward(sid_at(-2 * W))

    wait(pfull_v.at[pl.ds(0, R - 1)], g_r.at[4])
    gram = -dot_t(inv_v[...], pfull_v[...].reshape(BLK, BLK))
    row = lax.broadcasted_iota(jnp.int32, (BLK, BLK), 0)
    col = lax.broadcasted_iota(jnp.int32, (BLK, BLK), 1)
    g_out[...] = jnp.where(row >= col, gram, jnp.zeros_like(gram))

    @pl.when(own)
    def _():
        wait(lc.at[pl.ds(0, R - 1)], sc_s)

    wait(lc.at[pl.ds(0, R - 1)], ag_s)
    wait(flip_in.at[pl.ds(0, R - 1)], fl_s)

    @pl.when(jnp.logical_not(to_self))
    def _():
        wait(route_src, rt_s)

    wait(half_v.at[pl.ds(0, Z - 1)], rs_s)
    wait(half_v.at[pl.ds(0, Z - 1)], x_s)
    wait(prod_in.at[pl.ds(0, R - 1)], g_s.at[0])
    if W > 1:
        wait(quad_in.at[pl.ds(0, W - 1)], g_s.at[1])
    wait(cross_in.at[pl.ds(0, 3)], g_s.at[2])
    wait(pfull_v.at[pl.ds(0, R - 1)], g_s.at[4])
    wait(half_v, xp_s)
    wait(half_v, xp_r)


def solution(mesh):
    R, C = mesh.shape["row"], mesh.shape["col"]
    Z = C // 2
    W = Z // 4
    SL = 8 * BLK // C
    NS = BLK // SL
    HALF = 4 * NS
    GL = BLK // R

    def per_device(trail_adjoint, panel, panel_adjoint, diag_block):
        hbm = pl.BlockSpec(memory_space=pltpu.MemorySpace.HBM)
        vmem = pl.BlockSpec(memory_space=pltpu.MemorySpace.VMEM)
        vm = lambda *shape: pltpu.VMEM(shape, F32)
        dma = pltpu.SemaphoreType.DMA
        in_hbm = lambda x: pltpu.with_memory_space_constraint(x, pltpu.MemorySpace.HBM)
        x, gram = pl.pallas_call(
            functools.partial(kernel, R, C),
            out_shape=(
                jax.ShapeDtypeStruct((2 * HALF, SL, BLK), F32),
                jax.ShapeDtypeStruct((BLK, BLK), F32),
            ),
            in_specs=[hbm] * 4,
            out_specs=(vmem, vmem),
            scratch_shapes=[
                vm(8, 4 * BLK, BLK),
                pltpu.VMEM((8 * BLK, 4 * BLK), BF16),
                pltpu.VMEM((8 * BLK, 4 * BLK), BF16),
                vm(2 * HALF, SL, BLK),
                vm(SL, BLK),
                vm(BLK, BLK),
                pltpu.VMEM((2 * BLK, 8 * BLK), BF16),
                vm(BLK, BLK),
                vm(R, SL, BLK),
                vm(R, SL, BLK),
                vm(R, SL, BLK),
                vm(SL, BLK),
                vm(SL, BLK),
                vm(HALF, SL, BLK),
                vm(HALF, SL, BLK),
                vm(HALF, SL, BLK),
                vm(W, SL, BLK),
                vm(max(W - 1, 1), SL, BLK),
                vm(2, SL, BLK),
                vm(2 * W, SL, BLK),
                vm(R, GL, BLK),
                vm(R, GL, BLK),
                vm(GL, BLK),
                vm(W, GL, BLK),
                vm(GL, BLK),
                vm(4, GL, BLK),
                vm(GL, BLK),
                vm(GL, BLK),
                vm(R, GL, BLK),
                dma((12,)),
                dma(()),
                dma(()),
                dma(()),
                dma(()),
                dma(()),
                dma(()),
                dma(()),
                dma(()),
                dma(()),
                dma(()),
                dma(()),
                dma((3,)),
                dma(()),
                dma((4 * W,)),
                dma(()),
                dma(()),
                dma((5,)),
                dma((5,)),
            ],
            compiler_params=pltpu.CompilerParams(
                collective_id=0, has_side_effects=True, vmem_limit_bytes=32 * 1024 * 1024
            ),
        )(
            in_hbm(trail_adjoint.reshape(8, 4 * BLK, BLK)),
            in_hbm(panel.reshape(2 * HALF, SL, BLK)),
            in_hbm(panel_adjoint.reshape(2 * HALF, SL, BLK)),
            in_hbm(diag_block),
        )
        return x.reshape(8, BLK, BLK), gram

    return jax.shard_map(
        per_device,
        mesh=mesh,
        in_specs=(P(None, "row", None, "col"), P(None, "row", None), P(None, "row", None), P()),
        out_specs=(P(None, "row", None), P()),
        check_vma=False,
    )
```

time: 64.6 us -> 59.3 us (0.918)
  local copies, waits for them, and re-layouts: 5.93 us -> 1.42 us
  Pallas kernels: 57.8 us -> 57 us
    unnamed x10 -> x2, local copies, waits for them, and re-layouts: 5.93 us -> 1.42 us
    pallas_call x1, Pallas kernels: 57.8 us -> 57 us  [per_device(): pl.pallas_call(functools.partial(kernel, R, C), out_shape=(jax.ShapeDtype...]
where the time goes in v2:
time: 59.3 us; the launch traced here: 59.1 us
  Pallas kernels  57 us (96%)
  local copies, waits for them, and re-layouts  1.42 us (2%)
  between operations  0.64 us (1%)
    pallas_call x1, Pallas kernels, per_device(): pl.pallas_call(functools.partial(kernel, R, C), out_shape=(jax.ShapeDtype...  57 us
    unnamed x2, local copies, waits for them, and re-layouts  1.42 us

profile of v2, /device:TPU:1, one launch (start us, length us, event | category | flops | bytes accessed | tf_op | source)
XLA Modules:
  0.0 59.1 jit_solution(14345150393271646219)
XLA Ops:
  0.6 57.0 %shard_map.59 = (f32[32,32,128]{2,1,0:T(8,128)S(1)}, f32[128,128]{1,0:T(8,128)S(1)}) custom-call(f32[8,512,128]{2,1,0:T(8,128)} %bitcast.5, f32[32,32,128]{2,1,0:T(8,128)} %bitcast.6, f32[32,32,128]{2,1,0:T(8,128)} %bitcast.7, f32[128,128]{1,0:T(8,128)} %diag_hbm.1), custom_call_target="tpu_custom_call" | custom-call | tf_op jit(solution)/shard_map/pallas_call | solution.py:431
  57.7 0.8 %copy.8 = f32[8,128,128]{2,1,0:T(8,128)} copy(f32[8,128,128]{2,1,0:T(8,128)S(1)} %bitcast.4) | data formatting | bytes 1048576
  58.5 0.6 %copy.9 = f32[128,128]{1,0:T(8,128)} copy(f32[128,128]{1,0:T(8,128)S(1)} %get-tuple-element.9) | data formatting | bytes 131072

commit v3 on v2

--- a/solution.py
+++ b/solution.py
@@ -1,4 +1,5 @@
 import functools
+import math
 
 import jax
 import jax.numpy as jnp
@@ -12,6 +13,7 @@
 BF16 = jnp.bfloat16
 HI = lax.Precision.HIGHEST
 BLK = 128
+DELAY = 800
 
 
 def dot(a, b):
@@ -121,6 +123,7 @@
     NS = BLK // SL
     HALF = 4 * NS
     HR = 4 * BLK
+    side = math.isqrt(R)
     r = lax.axis_index("row")
     c = lax.axis_index("col")
     z = c // 2
@@ -129,11 +132,21 @@
     def dev(row, chip, core):
         return (row, chip * 2 + core)
 
-    def plane(i):
-        return ((r + i) & (R - 1), c)
+    hops = lambda d: min(d, side - d)
+    steps = [(dx, dy) for dx in range(side) for dy in range(side) if dx + dy > 0]
+    steps.sort(key=lambda d: -(hops(d[0]) + hops(d[1])))
+
+    def at(step):
+        dx, dy = step
+        return ((r // side + dx) & (side - 1)) * side + ((r + dy) & (side - 1))
+
+    sign = 1 - 2 * k
+
+    def away(delta):
+        return (z + sign * delta) & (Z - 1)
 
     def chip(delta):
-        return dev(r, (z + delta) & (Z - 1), k)
+        return dev(r, away(delta), k)
 
     def copy(src, dst, send, recv, device):
         return pltpu.make_async_remote_copy(
@@ -156,13 +169,13 @@
         return (2 * (m // NS) + o // (R // 2)) * NS + (m & (NS - 1))
 
     def slice_for(delta):
-        return slice_in_half(offset_of(r, (z + delta) & (Z - 1)))
+        return slice_in_half(offset_of(r, away(delta)))
 
     barrier = pltpu.get_barrier_semaphore()
     other = dev(r, z, 1 - k)
-    for i in range(1, R):
-        pl.semaphore_signal(barrier, inc=1, device_id=plane(i), device_id_type=MESH)
-    for i in range(1, W + 1):
+    for step in steps:
+        pl.semaphore_signal(barrier, inc=1, device_id=(at(step), c), device_id_type=MESH)
+    for i in range(W, 0, -1):
         for delta in (i, -i):
             for core in (0, 1):
                 near_by = dev(r, (z + delta) & (Z - 1), core)
@@ -192,9 +205,9 @@
 
     @pl.when(own)
     def _():
-        for i in range(1, R):
-            s = (r + i) & (R - 1)
-            copy(piece(s), lc.at[s], sc_s, sc_r, plane(i)).start()
+        for step in steps:
+            s = at(step)
+            copy(piece(s), lc.at[s], sc_s, sc_r, (s, c)).start()
         mine = pltpu.make_async_copy(piece(r), lc.at[r], loc.at[11])
         mine.start()
         mine.wait()
@@ -216,15 +229,15 @@
         both = bdot(pt_v[...], s_hi[:, wide])
         part = both[:BLK] + (both[BLK:] + bdot(pt_v[pl.ds(0, BLK), :], s_lo[:, wide]))
         flip_v[pl.ds(b * 2 * NS, 2 * NS)] = part.T.reshape(2 * NS, SL, BLK)
-    for i in range(1, R):
-        copy(flip_v.at[(r + i) & (R - 1)], flip_in.at[r], fl_s, fl_r, plane(i)).start()
+    for step in steps:
+        copy(flip_v.at[at(step)], flip_in.at[r], fl_s, fl_r, (at(step), c)).start()
 
     @pl.when(jnp.logical_not(own))
     def _():
         wait(lc.at[r], sc_r)
 
-    for i in range(1, R):
-        copy(lc.at[r], lc.at[r], ag_s, ag_r, plane(i)).start()
+    for step in steps:
+        copy(lc.at[r], lc.at[r], ag_s, ag_r, (at(step), c)).start()
 
     cp_d.wait()
     inv_v[...] = invert_lower(d_v[...])
@@ -236,6 +249,13 @@
         total_flip = total_flip + flip_in[i]
     route_src[...] = total_flip
 
+    cross_part = dot_t(total_flip, lc[r])
+    cp_b.wait()
+    prod = dot_t(b_v[...], p_v[sid]) - (cross_part + cross_part.T)
+    prod_v[...] = prod.reshape(R, BLK // R, BLK)
+    for step in steps:
+        copy(prod_v.at[at(step)], prod_in.at[r], g_s.at[0], g_r.at[0], (at(step), c)).start()
+
     wait(lc.at[pl.ds(0, R - 1)], ag_r)
 
     to_r = owner
@@ -264,7 +284,6 @@
     pair = copy(give_v, pair_in, pr_s, pr_r, other)
     pair.start()
     kept = direct_half(k)
-    kept_hi, kept_lo = split(kept.reshape(HR, BLK))
     pair.wait()
     half_v[...] = kept + pair_in[...]
 
@@ -274,22 +293,20 @@
             copy(
                 half_v.at[slice_for(-d)], agg_near.at[d - W - 1], rs_s, rs_r.at[1], chip(W - d)
             ).start()
+
+    wait(prod_in.at[pl.ds(0, R - 1)], g_r.at[0])
+    prod_in[r] = prod_v[r]
+    acc = prod_in[0]
+    for i in range(1, R):
+        acc = acc + prod_in[i]
+    group, lane = z // W, z & (W - 1)
+    quad_v[...] = acc
+    for i in range(1, W):
+        mate = dev(r, group * W + ((lane + i) & (W - 1)), k)
+        copy(quad_v, quad_in.at[lane], g_s.at[1], g_r.at[1], mate).start()
     for d in range(W - 1, 0, -1):
         copy(half_v.at[slice_for(d)], fin_in.at[d - 1], rs_s, rs_r.at[2], chip(d)).start()
         copy(half_v.at[slice_for(-d)], fin_in.at[W + d - 2], rs_s, rs_r.at[2], chip(-d)).start()
-
-    def product(base, hi, lo):
-        at = pl.ds(pl.multiple_of(base * HR, HR), HR)
-        both = bdot(pt_v[:, at], hi)
-        return both[:BLK] + (both[BLK:] + bdot(pt_v[pl.ds(0, BLK), at], lo))
-
-    give_hi, give_lo = split(give_v[...].reshape(HR, BLK))
-    own_sum = product(k, kept_hi, kept_lo) + product(1 - k, give_hi, give_lo)
-    cp_b.wait()
-    prod = dot_t(b_v[...], p_v[sid]) - (own_sum + own_sum.T)
-    prod_v[...] = prod.reshape(R, BLK // R, BLK)
-    for i in range(1, R):
-        copy(prod_v.at[(r + i) & (R - 1)], prod_in.at[r], g_s.at[0], g_r.at[0], plane(i)).start()
 
     wait(agg_far, rs_r.at[0])
     far = half_v[slice_for(W)]
@@ -305,42 +322,6 @@
     agg_out[1] = near
     copy(agg_out.at[1], fin_in.at[2 * W - 1], rs_s, rs_r.at[2], chip(-W)).start()
 
-    wait(prod_in.at[pl.ds(0, R - 1)], g_r.at[0])
-    prod_in[r] = prod_v[r]
-    acc = prod_in[0]
-    for i in range(1, R):
-        acc = acc + prod_in[i]
-    group, lane = z // W, z & (W - 1)
-    quad_v[...] = acc
-    for i in range(1, W):
-        mate = dev(r, group * W + ((lane + i) & (W - 1)), k)
-        copy(quad_v, quad_in.at[lane], g_s.at[1], g_r.at[1], mate).start()
-
-    @pl.when(jnp.logical_not(to_self))
-    def _():
-        wait(route_in, rt_r)
-
-    wait(fin_in, rs_r.at[2])
-    total = half_v[my_slice]
-    for i in range(2 * W):
-        total = total + fin_in[i]
-    total = b_v[...] - (total + route_in[...])
-    x_v[sid] = dot(total, inv_v[...])
-
-    def sid_at(delta):
-        return k * HALF + slice_for(delta)
-
-    def send_x(s, sem, device):
-        copy(x_v.at[s], x_v.at[s], x_s, x_r.at[sem], device).start()
-
-    def forward(s):
-        copy(x_v.at[s], x_v.at[s], xp_s, xp_r, other).start()
-
-    for d in range(W, 0, -1):
-        send_x(sid, d, chip(d))
-        send_x(sid, 2 * W + d, chip(-d))
-    forward(sid)
-
     if W > 1:
         wait(quad_in.at[pl.ds(0, W - 1)], g_r.at[1])
     quad_in[lane] = quad_v[...]
@@ -350,6 +331,34 @@
     cross_v[...] = acc
     for i in range(1, 4):
         copy(cross_v, cross_in.at[group], g_s.at[2], g_r.at[2], chip(i * W)).start()
+
+    @pl.when(jnp.logical_not(to_self))
+    def _():
+        wait(route_in, rt_r)
+
+    wait(fin_in, rs_r.at[2])
+    total = half_v[my_slice]
+    for i in range(2 * W):
+        total = total + fin_in[i]
+    total = b_v[...] - (total + route_in[...])
+    x_v[sid] = dot(total, inv_v[...])
+
+    def sid_at(delta):
+        return k * HALF + slice_for(delta)
+
+    def send_x(s, sem, device):
+        copy(x_v.at[s], x_v.at[s], x_s, x_r.at[sem], device).start()
+
+    def forward(s):
+        copy(x_v.at[s], x_v.at[s], xp_s, xp_r, other).start()
+
+    send_x(sid, W, chip(W))
+    send_x(sid, 3 * W, chip(-W))
+    forward(sid)
+    pl.delay(DELAY)
+    for d in range(W - 1, 0, -1):
+        send_x(sid, d, chip(d))
+        send_x(sid, 2 * W + d, chip(-d))
 
     far_sid = sid_at(-W)
     wait(x_v.at[far_sid], x_r.at[W])
@@ -374,8 +383,8 @@
     hand.start()
     hand.wait()
     pfull_v[r] = ppair_v[...] + ppair_in[...]
-    for i in range(1, R):
-        copy(pfull_v.at[r], pfull_v.at[r], g_s.at[4], g_r.at[4], plane(i)).start()
+    for step in steps:
+        copy(pfull_v.at[r], pfull_v.at[r], g_s.at[4], g_r.at[4], (at(step), c)).start()
 
     for d in range(1, W):
         wait(x_v.at[sid_at(-W - d)], x_r.at[W + d])

time: 59.3 us -> 54.1 us (0.912)
  Pallas kernels: 57 us -> 51.8 us
    pallas_call x1, Pallas kernels: 57 us -> 51.8 us  [per_device(): pl.pallas_call(functools.partial(kernel, R, C), out_shape=(jax.ShapeDtype...]
where the time goes in v3:
time: 54.1 us; the launch traced here: 53.9 us
  Pallas kernels  51.8 us (96%)
  local copies, waits for them, and re-layouts  1.42 us (3%)
  between operations  0.64 us (1%)
    pallas_call x1, Pallas kernels, per_device(): pl.pallas_call(functools.partial(kernel, R, C), out_shape=(jax.ShapeDtype...  51.8 us
    unnamed x2, local copies, waits for them, and re-layouts  1.42 us

profile of v3, /device:TPU:1, one launch (start us, length us, event | category | flops | bytes accessed | tf_op | source)
XLA Modules:
  0.0 53.9 jit_solution(11432105480728535095)
XLA Ops:
  0.6 51.8 %shard_map.59 = (f32[32,32,128]{2,1,0:T(8,128)S(1)}, f32[128,128]{1,0:T(8,128)S(1)}) custom-call(f32[8,512,128]{2,1,0:T(8,128)} %bitcast.5, f32[32,32,128]{2,1,0:T(8,128)} %bitcast.6, f32[32,32,128]{2,1,0:T(8,128)} %bitcast.7, f32[128,128]{1,0:T(8,128)} %diag_hbm.1), custom_call_target="tpu_custom_call" | custom-call | tf_op jit(solution)/shard_map/pallas_call | solution.py:440
  52.5 0.8 %copy.8 = f32[8,128,128]{2,1,0:T(8,128)} copy(f32[8,128,128]{2,1,0:T(8,128)S(1)} %bitcast.4) | data formatting | bytes 1048576
  53.3 0.6 %copy.9 = f32[128,128]{1,0:T(8,128)} copy(f32[128,128]{1,0:T(8,128)S(1)} %get-tuple-element.9) | data formatting | bytes 131072

commit v4 on v3

--- a/solution.py
+++ b/solution.py
@@ -13,7 +13,8 @@
 BF16 = jnp.bfloat16
 HI = lax.Precision.HIGHEST
 BLK = 128
-DELAY = 800
+RS_PAUSE = 400
+AG_PAUSE = 600
 
 
 def dot(a, b):
@@ -294,6 +295,11 @@
                 half_v.at[slice_for(-d)], agg_near.at[d - W - 1], rs_s, rs_r.at[1], chip(W - d)
             ).start()
 
+    pl.delay(RS_PAUSE)
+    for d in range(W - 1, 0, -1):
+        copy(half_v.at[slice_for(d)], fin_in.at[d - 1], rs_s, rs_r.at[2], chip(d)).start()
+        copy(half_v.at[slice_for(-d)], fin_in.at[W + d - 2], rs_s, rs_r.at[2], chip(-d)).start()
+
     wait(prod_in.at[pl.ds(0, R - 1)], g_r.at[0])
     prod_in[r] = prod_v[r]
     acc = prod_in[0]
@@ -304,9 +310,6 @@
     for i in range(1, W):
         mate = dev(r, group * W + ((lane + i) & (W - 1)), k)
         copy(quad_v, quad_in.at[lane], g_s.at[1], g_r.at[1], mate).start()
-    for d in range(W - 1, 0, -1):
-        copy(half_v.at[slice_for(d)], fin_in.at[d - 1], rs_s, rs_r.at[2], chip(d)).start()
-        copy(half_v.at[slice_for(-d)], fin_in.at[W + d - 2], rs_s, rs_r.at[2], chip(-d)).start()
 
     wait(agg_far, rs_r.at[0])
     far = half_v[slice_for(W)]
@@ -355,10 +358,16 @@
     send_x(sid, W, chip(W))
     send_x(sid, 3 * W, chip(-W))
     forward(sid)
-    pl.delay(DELAY)
+    pl.delay(AG_PAUSE)
     for d in range(W - 1, 0, -1):
         send_x(sid, d, chip(d))
         send_x(sid, 2 * W + d, chip(-d))
+
+    wait(cross_in.at[pl.ds(0, 3)], g_r.at[2])
+    cross_in[group] = cross_v[...]
+    ppair_v[...] = (cross_in[0] + cross_in[1]) + (cross_in[2] + cross_in[3])
+    hand = copy(ppair_v, ppair_in, g_s.at[3], g_r.at[3], other)
+    hand.start()
 
     far_sid = sid_at(-W)
     wait(x_v.at[far_sid], x_r.at[W])
@@ -368,6 +377,11 @@
     wait(x_v.at[near_sid], x_r.at[3 * W])
     for d in range(W - 1, 0, -1):
         send_x(near_sid, 3 * W + d, chip(-d))
+    hand.wait()
+    pfull_v[r] = ppair_v[...] + ppair_in[...]
+    for step in steps:
+        copy(pfull_v.at[r], pfull_v.at[r], g_s.at[4], g_r.at[4], (at(step), c)).start()
+
     forward(far_sid)
     forward(near_sid)
     for d in range(1, W):
@@ -375,16 +389,6 @@
         forward(sid_at(-d))
         wait(x_v.at[sid_at(d)], x_r.at[2 * W + d])
         forward(sid_at(d))
-
-    wait(cross_in.at[pl.ds(0, 3)], g_r.at[2])
-    cross_in[group] = cross_v[...]
-    ppair_v[...] = (cross_in[0] + cross_in[1]) + (cross_in[2] + cross_in[3])
-    hand = copy(ppair_v, ppair_in, g_s.at[3], g_r.at[3], other)
-    hand.start()
-    hand.wait()
-    pfull_v[r] = ppair_v[...] + ppair_in[...]
-    for step in steps:
-        copy(pfull_v.at[r], pfull_v.at[r], g_s.at[4], g_r.at[4], (at(step), c)).start()
 
     for d in range(1, W):
         wait(x_v.at[sid_at(-W - d)], x_r.at[W + d])
@@ -422,6 +426,15 @@
     wait(half_v, xp_r)
 
 
+def write_out(x_v, g_v, x_hbm, g_hbm, sem):
+    g_copy = pltpu.make_async_copy(g_v, g_hbm, sem.at[0])
+    g_copy.start()
+    x_copy = pltpu.make_async_copy(x_v, x_hbm, sem.at[1])
+    x_copy.start()
+    g_copy.wait()
+    x_copy.wait()
+
+
 def solution(mesh):
     R, C = mesh.shape["row"], mesh.shape["col"]
     Z = C // 2
@@ -432,6 +445,7 @@
     GL = BLK // R
 
     def per_device(trail_adjoint, panel, panel_adjoint, diag_block):
+        any_spec = pl.BlockSpec(memory_space=pl.ANY)
         hbm = pl.BlockSpec(memory_space=pltpu.MemorySpace.HBM)
         vmem = pl.BlockSpec(memory_space=pltpu.MemorySpace.VMEM)
         vm = lambda *shape: pltpu.VMEM(shape, F32)
@@ -504,6 +518,17 @@
             in_hbm(panel_adjoint.reshape(2 * HALF, SL, BLK)),
             in_hbm(diag_block),
         )
+        x, gram = pl.pallas_call(
+            write_out,
+            out_shape=(
+                jax.ShapeDtypeStruct((2 * HALF, SL, BLK), F32),
+                jax.ShapeDtypeStruct((BLK, BLK), F32),
+            ),
+            in_specs=[any_spec] * 2,
+            out_specs=(hbm, hbm),
+            scratch_shapes=[dma((2,))],
+            compiler_params=pltpu.CompilerParams(vmem_limit_bytes=8 * 1024 * 1024),
+        )(x, gram)
         return x.reshape(8, BLK, BLK), gram
 
     return jax.shard_map(

time: 54.1 us -> 53.1 us (0.982)
  local copies, waits for them, and re-layouts: 1.42 us -> 0 us
    unnamed x2 -> x0, local copies, waits for them, and re-layouts: 1.42 us -> none
    pallas_call x0 -> x1, Pallas kernels: none -> 0.83 us  [per_device(): pl.pallas_call(write_out, out_shape=(jax.ShapeDtypeStruct((2 * HALF, SL,...]
where the time goes in v4:
time: 53.1 us; the launch traced here: 53 us
  Pallas kernels  52.3 us (98%)
  between operations  0.64 us (1%)
    pallas_call x1, Pallas kernels, per_device(): pl.pallas_call(functools.partial(kernel, R, C), out_shape=(jax.ShapeDtype...  51.5 us

profile of v4, /device:TPU:1, one launch (start us, length us, event | category | flops | bytes accessed | tf_op | source)
XLA Modules:
  0.0 53.0 jit_solution(302181245941386057)
XLA Ops:
  0.6 51.5 %shard_map.59 = (f32[32,32,128]{2,1,0:T(8,128)S(1)}, f32[128,128]{1,0:T(8,128)S(1)}) custom-call(f32[8,512,128]{2,1,0:T(8,128)} %bitcast.4, f32[32,32,128]{2,1,0:T(8,128)} %bitcast.5, f32[32,32,128]{2,1,0:T(8,128)} %bitcast.6, f32[128,128]{1,0:T(8,128)} %diag_hbm.1), custom_call_target="tpu_custom_call" | custom-call | tf_op jit(solution)/shard_map/pallas_call | solution.py:454
  52.1 0.8 %shard_map.60 = (f32[32,32,128]{2,1,0:T(8,128)}, f32[128,128]{1,0:T(8,128)}) custom-call(f32[32,32,128]{2,1,0:T(8,128)S(1)} %get-tuple-element.6.x_v, f32[128,128]{1,0:T(8,128)S(1)} %get-tuple-element.7.g_v), custom_call_target="tpu_custom_call" | custom-call | tf_op jit(solution)/shard_map/pallas_call | solution.py:521

commit v5 on v4

--- a/solution.py
+++ b/solution.py
@@ -195,8 +195,7 @@
     cp_d = pltpu.make_async_copy(diag_hbm, d_v, loc.at[10])
     cp_d.start()
 
-    pl.semaphore_wait(barrier, R - 1 + 4 * W + 1)
-
+    greeted = R - 1 + 4 * W + 1
     owner = c & (R - 1)
     which = c // R
     own = owner == r
@@ -206,6 +205,7 @@
 
     @pl.when(own)
     def _():
+        pl.semaphore_wait(barrier, greeted)
         for step in steps:
             s = at(step)
             copy(piece(s), lc.at[s], sc_s, sc_r, (s, c)).start()
@@ -230,6 +230,11 @@
         both = bdot(pt_v[...], s_hi[:, wide])
         part = both[:BLK] + (both[BLK:] + bdot(pt_v[pl.ds(0, BLK), :], s_lo[:, wide]))
         flip_v[pl.ds(b * 2 * NS, 2 * NS)] = part.T.reshape(2 * NS, SL, BLK)
+
+    @pl.when(jnp.logical_not(own))
+    def _():
+        pl.semaphore_wait(barrier, greeted)
+
     for step in steps:
         copy(flip_v.at[at(step)], flip_in.at[r], fl_s, fl_r, (at(step), c)).start()
 

time: 53.1 us -> 52.3 us (0.985)
  Pallas kernels: 52.3 us -> 51.5 us
    pallas_call x1, Pallas kernels: 51.5 us -> 50.7 us  [per_device(): pl.pallas_call(functools.partial(kernel, R, C), out_shape=(jax.ShapeDtype...]
where the time goes in v5:
time: 52.3 us; the launch traced here: 52.2 us
  Pallas kernels  51.5 us (98%)
  between operations  0.64 us (1%)
    pallas_call x1, Pallas kernels, per_device(): pl.pallas_call(functools.partial(kernel, R, C), out_shape=(jax.ShapeDtype...  50.7 us

profile of v5, /device:TPU:1, one launch (start us, length us, event | category | flops | bytes accessed | tf_op | source)
XLA Modules:
  0.0 52.2 jit_solution(10513018181141391538)
XLA Ops:
  0.6 50.7 %shard_map.59 = (f32[32,32,128]{2,1,0:T(8,128)S(1)}, f32[128,128]{1,0:T(8,128)S(1)}) custom-call(f32[8,512,128]{2,1,0:T(8,128)} %bitcast.4, f32[32,32,128]{2,1,0:T(8,128)} %bitcast.5, f32[32,32,128]{2,1,0:T(8,128)} %bitcast.6, f32[128,128]{1,0:T(8,128)} %diag_hbm.1), custom_call_target="tpu_custom_call" | custom-call | tf_op jit(solution)/shard_map/pallas_call | solution.py:459
  51.3 0.8 %shard_map.60 = (f32[32,32,128]{2,1,0:T(8,128)}, f32[128,128]{1,0:T(8,128)}) custom-call(f32[32,32,128]{2,1,0:T(8,128)S(1)} %get-tuple-element.6.x_v, f32[128,128]{1,0:T(8,128)S(1)} %get-tuple-element.7.g_v), custom_call_target="tpu_custom_call" | custom-call | tf_op jit(solution)/shard_map/pallas_call | solution.py:526

commit v6 on v5

--- a/solution.py
+++ b/solution.py
@@ -13,6 +13,7 @@
 BF16 = jnp.bfloat16
 HI = lax.Precision.HIGHEST
 BLK = 128
+FIRST = 1
 RS_PAUSE = 400
 AG_PAUSE = 600
 
@@ -111,6 +112,7 @@
     rs_s,
     rs_r,
     x_s,
+    x_d,
     x_r,
     xp_s,
     xp_r,
@@ -360,8 +362,22 @@
     def forward(s):
         copy(x_v.at[s], x_v.at[s], xp_s, xp_r, other).start()
 
+    chosen = []
+
+    def send_if(cond, s, sem, device):
+        one = copy(x_v.at[s], x_v.at[s], x_d.at[len(chosen)], x_r.at[sem], device)
+        chosen.append((cond, one))
+
+        @pl.when(cond)
+        def _():
+            one.start()
+
     send_x(sid, W, chip(W))
     send_x(sid, 3 * W, chip(-W))
+    for d in range(2 * W, W, -1):
+        send_if(away(d) < FIRST, sid, d, chip(d))
+        if d < 2 * W:
+            send_if(away(-d) < FIRST, sid, 2 * W + d, chip(-d))
     forward(sid)
     pl.delay(AG_PAUSE)
     for d in range(W - 1, 0, -1):
@@ -377,11 +393,11 @@
     far_sid = sid_at(-W)
     wait(x_v.at[far_sid], x_r.at[W])
     for d in range(W, 0, -1):
-        send_x(far_sid, W + d, chip(d))
+        send_if(away(d) >= FIRST, far_sid, W + d, chip(d))
     near_sid = sid_at(W)
     wait(x_v.at[near_sid], x_r.at[3 * W])
     for d in range(W - 1, 0, -1):
-        send_x(near_sid, 3 * W + d, chip(-d))
+        send_if(away(-d) >= FIRST, near_sid, 3 * W + d, chip(-d))
     hand.wait()
     pfull_v[r] = ppair_v[...] + ppair_in[...]
     for step in steps:
@@ -421,7 +437,9 @@
         wait(route_src, rt_s)
 
     wait(half_v.at[pl.ds(0, Z - 1)], rs_s)
-    wait(half_v.at[pl.ds(0, Z - 1)], x_s)
+    wait(half_v.at[pl.ds(0, 2 * W)], x_s)
+    for cond, one in chosen:
+        pl.when(cond)(one.wait_send)
     wait(prod_in.at[pl.ds(0, R - 1)], g_s.at[0])
     if W > 1:
         wait(quad_in.at[pl.ds(0, W - 1)], g_s.at[1])
@@ -508,6 +526,7 @@
                 dma(()),
                 dma((3,)),
                 dma(()),
+                dma((4 * W - 2,)),
                 dma((4 * W,)),
                 dma(()),
                 dma(()),

time: 52.3 us -> 51.6 us (0.987); the launches traced: 52.2 us -> 50.9 us
  Pallas kernels: 51.5 us -> 50.3 us
    pallas_call x1, Pallas kernels: 50.7 us -> 49.4 us  [per_device(): pl.pallas_call(functools.partial(kernel, R, C), out_shape=(jax.ShapeDtype...]
where the time goes in v6:
time: 51.6 us; the launch traced here: 50.9 us
  Pallas kernels  50.3 us (97%)
  between operations  0.64 us (1%)
    pallas_call x1, Pallas kernels, per_device(): pl.pallas_call(functools.partial(kernel, R, C), out_shape=(jax.ShapeDtype...  49.4 us

profile of v6, /device:TPU:1, one launch (start us, length us, event | category | flops | bytes accessed | tf_op | source)
XLA Modules:
  0.0 50.9 jit_solution(7392009929632380569)
XLA Ops:
  0.6 49.4 %shard_map.59 = (f32[32,32,128]{2,1,0:T(8,128)S(1)}, f32[128,128]{1,0:T(8,128)S(1)}) custom-call(f32[8,512,128]{2,1,0:T(8,128)} %bitcast.4, f32[32,32,128]{2,1,0:T(8,128)} %bitcast.5, f32[32,32,128]{2,1,0:T(8,128)} %bitcast.6, f32[128,128]{1,0:T(8,128)} %diag_hbm.1), custom_call_target="tpu_custom_call" | custom-call | tf_op jit(solution)/shard_map/pallas_call | solution.py:477
  50.1 0.8 %shard_map.60 = (f32[32,32,128]{2,1,0:T(8,128)}, f32[128,128]{1,0:T(8,128)}) custom-call(f32[32,32,128]{2,1,0:T(8,128)S(1)} %get-tuple-element.6.x_v, f32[128,128]{1,0:T(8,128)S(1)} %get-tuple-element.7.g_v), custom_call_target="tpu_custom_call" | custom-call | tf_op jit(solution)/shard_map/pallas_call | solution.py:545

commit v7 on v6

--- a/solution.py
+++ b/solution.py
@@ -77,6 +77,7 @@
     d_v,
     pt_v,
     inv_v,
+    inv_b,
     lc,
     flip_v,
     flip_in,
@@ -249,6 +250,9 @@
 
     cp_d.wait()
     inv_v[...] = invert_lower(d_v[...])
+    inv_hi, inv_lo = split(inv_v[...])
+    inv_b[:, pl.ds(0, BLK)] = inv_hi
+    inv_b[:, pl.ds(BLK, BLK)] = inv_lo
 
     wait(flip_in.at[pl.ds(0, R - 1)], fl_r)
     flip_in[r] = flip_v[r]
@@ -351,7 +355,9 @@
     for i in range(2 * W):
         total = total + fin_in[i]
     total = b_v[...] - (total + route_in[...])
-    x_v[sid] = dot(total, inv_v[...])
+    t_hi, t_lo = split(total)
+    both = bdot(t_hi, inv_b[...])
+    x_v[sid] = both[:, :BLK] + (both[:, BLK:] + bdot(t_lo, inv_b[:, pl.ds(0, BLK)]))
 
     def sid_at(delta):
         return k * HALF + slice_for(delta)
@@ -491,6 +497,7 @@
                 vm(BLK, BLK),
                 pltpu.VMEM((2 * BLK, 8 * BLK), BF16),
                 vm(BLK, BLK),
+                pltpu.VMEM((BLK, 2 * BLK), BF16),
                 vm(R, SL, BLK),
                 vm(R, SL, BLK),
                 vm(R, SL, BLK),

time: 51.6 us -> 51.6 us (level)
  no operation moved by 1% of the time
where the time goes in v7:
time: 51.6 us; the launch traced here: 50.9 us
  Pallas kernels  50.3 us (97%)
  between operations  0.64 us (1%)
    pallas_call x1, Pallas kernels, per_device(): pl.pallas_call(functools.partial(kernel, R, C), out_shape=(jax.ShapeDtype...  49.5 us

profile of v7, /device:TPU:1, one launch (start us, length us, event | category | flops | bytes accessed | tf_op | source)
XLA Modules:
  0.0 50.9 jit_solution(16914930331190607494)
XLA Ops:
  0.6 49.5 %shard_map.59 = (f32[32,32,128]{2,1,0:T(8,128)S(1)}, f32[128,128]{1,0:T(8,128)S(1)}) custom-call(f32[8,512,128]{2,1,0:T(8,128)} %bitcast.4, f32[32,32,128]{2,1,0:T(8,128)} %bitcast.5, f32[32,32,128]{2,1,0:T(8,128)} %bitcast.6, f32[128,128]{1,0:T(8,128)} %diag_hbm.1), custom_call_target="tpu_custom_call" | custom-call | tf_op jit(solution)/shard_map/pallas_call | solution.py:483
  50.1 0.8 %shard_map.60 = (f32[32,32,128]{2,1,0:T(8,128)}, f32[128,128]{1,0:T(8,128)}) custom-call(f32[32,32,128]{2,1,0:T(8,128)S(1)} %get-tuple-element.6.x_v, f32[128,128]{1,0:T(8,128)S(1)} %get-tuple-element.7.g_v), custom_call_target="tpu_custom_call" | custom-call | tf_op jit(solution)/shard_map/pallas_call | solution.py:552
